TPU v7x, 32 devices: a whole 2x2x4 slice. The times are simulated.
32 devices in a mesh: groups: 2 (over y), expert: 4 (over z), dp: 2 (over x), inner: 2 (over core).
Axes of the slice: x: 2, y: 2, z: 4, core: 2. Of those that a mesh axis runs over, the one named last changes fastest.
Arguments:
- tokens: bfloat16 [2048, 1536], P(('groups', 'expert', 'dp'), 'inner'), parts along dimension 0, may hold values from -6 to 6
- out_grad: bfloat16 [2048, 1536], P(('groups', 'expert', 'dp'), 'inner'), parts along dimension 0, may hold values from -6 to 6
- expert_ids: int32 [2048, 8], P(('groups', 'expert', 'dp')), parts along dimension 0, may hold values from 0 to 63, all different within a row; in each aligned block of 128 rows (0 to 127, 128 to 255, ...) at most 17 rows name the same one
- gate_probs: float32 [2048, 8], P(('groups', 'expert', 'dp')), parts along dimension 0, may hold values from 0.05 to 0.5
- gate_weight: bfloat16 [64, 1536, 384], P('expert', 'inner', 'dp'), may hold values from -0.15625 to 0.15625
- up_weight: bfloat16 [64, 1536, 384], P('expert', 'inner', 'dp'), may hold values from -0.15625 to 0.15625
- down_weight: bfloat16 [64, 384, 1536], P('expert', 'dp', 'inner'), may hold values from -0.3125 to 0.3125
Outputs:
- token_grad: bfloat16 [2048, 1536], P(('groups', 'expert', 'dp'), 'inner'), parts along dimension 0
- prob_grad: float32 [2048, 8], P(('groups', 'expert', 'dp')), parts along dimension 0
- gate_weight_grad: bfloat16 [128, 1536, 384], P(('groups', 'expert'), 'inner', 'dp'), parts along dimension 0
- up_weight_grad: bfloat16 [128, 1536, 384], P(('groups', 'expert'), 'inner', 'dp'), parts along dimension 0
- down_weight_grad: bfloat16 [128, 384, 1536], P(('groups', 'expert'), 'dp', 'inner'), parts along dimension 0
There are 2 independent parts, one for each index of `groups`. A program takes and returns all parts, laid end to end along the dimension named above; an argument that names none is the same for every part. Nothing has to cross between parts.
Inputs may be any that keep to these rules, and one draw needn't show every extreme that they name: `expert_ids`: within the rows of one block of 128 tokens no expert is chosen more than 17 times, and some expert is chosen exactly 17 times in some block; a token's 8 experts differ.
All inputs are finite; a program needn't handle non-finite values.
Results may differ from a plain program's by a relative error of at most 0.015.
Values may be sent and summed in bfloat16 or wider, within the bound.
A program may use at most 192 MiB of HBM per device.

v0:
```python
import jax
import jax.numpy as jnp
from jax import lax
from jax.sharding import PartitionSpec as P

F32 = jnp.float32
BF16 = jnp.bfloat16


def select_rows(packed, width, top_count, per_dev, block_rows, capacity):
    total = packed.shape[0]
    blocks = total // block_rows
    run = 4 if blocks % 4 == 0 else 1
    runs = blocks // run
    span = run * block_rows
    rows = -(-run * capacity // 16) * 16
    ids = packed[:, 2 * width : 2 * width + top_count].astype(jnp.int32)
    probs = packed[:, 2 * width + top_count : 2 * width + 2 * top_count]
    mine = lax.axis_index("expert") * per_dev + jnp.arange(per_dev, dtype=jnp.int32)
    hits = ids[:, :, None] == mine[None, None, :]
    member = jnp.any(hits, axis=1).reshape(runs, span, per_dev)
    weight = jnp.sum(jnp.where(hits, probs[:, :, None].astype(F32), 0.0), axis=1)
    weight = weight.reshape(runs, span, per_dev)
    at = jnp.arange(span, dtype=jnp.int32)
    earlier = (at[:, None] > at[None, :]).astype(BF16)
    slot = jnp.einsum("ts,gse->get", earlier, member.astype(BF16), preferred_element_type=F32)
    slot = jnp.where(member.transpose(0, 2, 1), slot.astype(jnp.int32), -1)
    places = jnp.arange(rows, dtype=jnp.int32)
    picked = slot[:, :, None, :] == places[None, None, :, None]
    row_prob = jnp.sum(jnp.where(picked, weight.transpose(0, 2, 1)[:, :, None, :], 0.0), axis=3)
    return (picked.astype(BF16), row_prob, hits, runs, span, rows)


def on_device(tokens, out_grad, expert_ids, gate_probs, gate_weight, up_weight, down_weight):
    tok_rows, width = tokens.shape
    top_count = expert_ids.shape[1]
    per_dev = gate_weight.shape[0]
    experts = per_dev * lax.axis_size("expert")
    capacity = tok_rows * top_count // experts + 1
    packed = jnp.concatenate(
        [tokens, out_grad, expert_ids.astype(BF16), gate_probs.astype(BF16)], axis=1
    )
    packed = lax.all_gather(packed, ("expert", "dp"), axis=0, tiled=True)
    picked, row_prob, hits, runs, span, rows = select_rows(
        packed, width, top_count, per_dev, tok_rows, capacity
    )
    both = packed[:, : 2 * width].reshape(runs, span, 2 * width)
    sorted_rows = jnp.einsum("gest,gtd->egsd", picked, both, preferred_element_type=F32)
    sorted_rows = sorted_rows.astype(BF16).reshape(per_dev, runs * rows, 2 * width)
    expert_rows, expert_grads = (sorted_rows[:, :, :width], sorted_rows[:, :, width:])
    prob_col = row_prob.transpose(1, 0, 2).reshape(per_dev, runs * rows, 1)
    hid = gate_weight.shape[2]
    parts = jnp.concatenate(
        [
            jnp.einsum("jrd,jdf->jrf", expert_rows, gate_weight, preferred_element_type=F32),
            jnp.einsum("jrd,jdf->jrf", expert_rows, up_weight, preferred_element_type=F32),
            jnp.einsum("jrd,jfd->jrf", expert_grads, down_weight, preferred_element_type=F32),
        ],
        axis=2,
    ).astype(BF16)
    sums = lax.psum(parts, "inner").astype(F32)
    gate, up, slope = (sums[..., :hid], sums[..., hid : 2 * hid], sums[..., 2 * hid :])
    sig = jax.nn.sigmoid(gate)
    act = gate * sig
    hidden = (act * up).astype(BF16)
    scores = jnp.sum(hidden.astype(F32) * slope, axis=-1)
    hidden_grad = prob_col * slope
    gate_back = (hidden_grad * up * sig * (1.0 + gate * (1.0 - sig))).astype(BF16)
    up_back = (hidden_grad * act).astype(BF16)
    row_grads = jnp.einsum("jrf,jdf->jrd", gate_back, gate_weight, preferred_element_type=F32)
    row_grads = (
        row_grads + jnp.einsum("jrf,jdf->jrd", up_back, up_weight, preferred_element_type=F32)
    ).astype(BF16)
    token_part = jnp.einsum(
        "gest,egsd->gtd",
        picked,
        row_grads.reshape(per_dev, runs, rows, width),
        preferred_element_type=F32,
    ).reshape(runs * span, width)
    score_rows = scores.reshape(per_dev, runs, rows).transpose(1, 0, 2)
    score_part = jnp.sum(picked.astype(F32) * score_rows[..., None], axis=2)
    score_part = score_part.transpose(0, 2, 1).reshape(runs * span, 1, per_dev)
    score_part = jnp.sum(jnp.where(hits, score_part, 0.0), axis=2)
    returned = lax.psum_scatter(
        jnp.concatenate([token_part, score_part], axis=1).astype(BF16),
        ("expert", "dp"),
        scatter_dimension=0,
        tiled=True,
    )
    grad_gate = jnp.einsum("jrd,jrf->jdf", expert_rows, gate_back, preferred_element_type=F32)
    grad_up = jnp.einsum("jrd,jrf->jdf", expert_rows, up_back, preferred_element_type=F32)
    down_rows = (prob_col * expert_grads.astype(F32)).astype(BF16)
    grad_down = jnp.einsum("jrf,jrd->jfd", hidden, down_rows, preferred_element_type=F32)
    return (
        returned[:, :width],
        returned[:, width:].astype(F32),
        grad_gate.astype(BF16),
        grad_up.astype(BF16),
        grad_down.astype(BF16),
    )


def solution(mesh):
    placed = (
        P(("groups", "expert", "dp"), "inner"),
        P(("groups", "expert", "dp"), "inner"),
        P(("groups", "expert", "dp"), None),
        P(("groups", "expert", "dp"), None),
        P("expert", "inner", "dp"),
        P("expert", "inner", "dp"),
        P("expert", "dp", "inner"),
    )
    return jax.shard_map(
        on_device,
        mesh=mesh,
        in_specs=placed,
        out_specs=(
            P(("groups", "expert", "dp"), "inner"),
            P(("groups", "expert", "dp"), None),
            P(("groups", "expert"), "inner", "dp"),
            P(("groups", "expert"), "inner", "dp"),
            P(("groups", "expert"), "dp", "inner"),
        ),
        check_vma=False,
    )
```

profile of v0, /device:TPU:0, one launch (start us, length us, event | category | flops | bytes accessed | tf_op | source)
XLA Modules:
  0.0 243.1 jit_solution(7060287537651137806)
XLA Ops:
  7.2 0.0 all-gather.2.cloned.1.call-start
  7.2 0.7 convert_element_type.69
  7.9 0.7 convert_element_type.68
  8.6 1.1 copy.65
  9.7 1.1 copy.64
  10.8 0.8 pad_maximum_fusion.2
  11.6 0.0 all-gather.2.cloned.1.call-update
  11.6 0.0 all-reduce.2.cloned.1.call-start
  11.6 66.2 %all-gather.2.cloned.1.call-done = bf16[1024,1552]{0,1:T(8,128)(2,1)} async-done(((bf16[128,1552]{0,1:T(8,128)(2,1)}), bf16[1024,1552]{0,1:T(8,128)(2,1)}) %all-gather.2.cloned.1.call-update) | async-done | bytes 3178512 | tf_op jit(solution)/shard_map/all_gather | solution.py:43
  77.9 0.7 slice_convert_fusion.1
  78.6 0.1 compare_reduce_fusion
  78.7 0.0 slice-start.2
  78.8 0.3 fusion.29
  79.0 1.6 slice-done.2
  80.6 2.9 %copy.79 = bf16[1024,1536]{1,0:T(8,128)(2,1)} copy(bf16[1024,1536]{0,1:T(8,128)(2,1)S(1)} %slice-done.2) | data formatting | bytes 6291456 | tf_op jit(solution)/shard_map/reshape | solution.py:47
  83.6 8.2 %convert_bitcast_fusion = bf16[16,2,80,1536]{3,2,0,1:T(8,128)(2,1)} fusion(bf16[2,512,1536,1]{2,1,3,0:T(8,128)(2,1)} %bitcast.58, s32[2,16,512]{2,1,0:T(8,128)S(1)} %fusion.29), kind=kOutput, calls=%fused_computation.2 | convolution fusion | flops 4031774720 | bytes 11075584 | tf_op jit(solution)/shard_map/gest,gtd->egsd/dot_general | solution.py:48
  91.8 3.7 %copy.71 = bf16[16,2,80,1536]{3,2,1,0:T(8,128)(2,1)S(1)} copy(bf16[16,2,80,1536]{3,2,0,1:T(8,128)(2,1)} %convert_bitcast_fusion) | data formatting | bytes 15728640 | tf_op jit(solution)/shard_map/convert_element_type | solution.py:49
  95.5 0.0 copy-start.1
  95.5 6.9 %fusion.26 = bf16[16,160,192]{2,1,0:T(8,128)(2,1)S(1)} fusion(bf16[16,192,768]{2,1,0:T(8,128)(2,1)} %param.13, bf16[16,160,1536]{2,1,0:T(8,128)(2,1)S(1)} %bitcast.47), kind=kOutput, calls=%fused_computation.36 | convolution fusion | flops 755466240 | bytes 9633792 | tf_op jit(solution)/shard_map/jrd,jfd->jrf/dot_general | solution.py:57
  102.5 4.1 %fusion.23 = bf16[16,160,192]{2,1,0:T(8,128)(2,1)S(1)} fusion(bf16[16,768,192]{1,2,0:T(8,128)(2,1)} %param.12, bf16[16,160,1536]{2,1,0:T(8,128)(2,1)S(1)} %bitcast.48), kind=kOutput, calls=%fused_computation.35 | convolution fusion | flops 755466240 | bytes 9633792 | tf_op jit(solution)/shard_map/jrd,jdf->jrf/dot_general | solution.py:56
  106.6 0.0 copy-done.1
  106.6 4.0 %fusion.20 = bf16[16,160,192]{2,1,0:T(8,128)(2,1)S(1)} fusion(bf16[16,768,192]{1,2,0:T(8,128)(2,1)} %param.11, bf16[16,160,1536]{2,1,0:T(8,128)(2,1)S(1)} %bitcast.49), kind=kOutput, calls=%fused_computation.34 | convolution fusion | flops 755466240 | bytes 9633792 | tf_op jit(solution)/shard_map/jrd,jdf->jrf/dot_general | solution.py:55
  110.6 2.8 %pad_maximum_fusion = bf16[16,160,576]{2,1,0:T(8,128)(2,1)} fusion(bf16[16,160,192]{2,1,0:T(8,128)(2,1)S(1)} %fusion.26, bf16[16,160,192]{2,1,0:T(8,128)(2,1)S(1)} %fusion.23, bf16[16,160,192]{2,1,0:T(8,128)(2,1)S(1)} %fusion.20), kind=kLoop, calls=%fused_computation.14 | loop fusion | flops 8847360 | bytes 5898240 | tf_op jit(solution)/shard_map/concatenate | solution.py:53
  113.4 0.0 all-reduce.2.cloned.1.call-update
  113.4 0.0 reduce-scatter.4.cloned.1.call-start
  113.5 0.1 fusion.32
  113.6 0.1 reshape.47
  113.7 21.5 %all-reduce.2.cloned.1.call-done = bf16[16,160,576]{2,1,0:T(8,128)(2,1)} async-done(((bf16[16,160,576]{2,1,0:T(8,128)(2,1)}), bf16[16,160,576]{2,1,0:T(8,128)(2,1)}) %all-reduce.2.cloned.1.call-update) | async-done | bytes 2949136 | tf_op jit(solution)/shard_map/psum | solution.py:61
  135.2 2.6 %convert_element_type.75 = f32[16,160,576]{2,1,0:T(8,128)S(1)} convert(bf16[16,160,576]{2,1,0:T(8,128)(2,1)} %all-reduce.2.cloned.1.call-done) | non-fusion elementwise | flops 1474560 | bytes 8847360 | tf_op jit(solution)/shard_map/convert_element_type | solution.py:61
  137.8 0.0 copy-start
  137.8 2.7 %multiply_reduce_fusion.1 = (f32[16,160]{1,0:T(8,128)S(1)}, bf16[16,160,192]{2,1,0:T(8,128)(2,1)}) fusion(f32[16,160,576]{2,1,0:T(8,128)S(1)} %convert_element_type.75), kind=kLoop, calls=%fused_computation.19 | loop fusion | flops 4421120 | bytes 6891520 | tf_op jit(solution)/shard_map/reduce_sum | solution.py:66
  140.6 0.4 copy-done
  141.0 0.1 reshape.52
  141.1 2.5 %select_reduce_fusion = (f32[2,16,80]{2,1,0:T(8,128)S(1)}, f32[2,16,512]{2,1,0:T(8,128)S(1)}) fusion(f32[2,16,512]{2,1,0:T(8,128)S(1)} %copy.68, s32[2,16,512]{2,1,0:T(8,128)S(1)} %fusion.29, f32[2,16,80]{2,1,0:T(8,128)S(1)} %copy.73), kind=kLoop, calls=%fused_computation.4 | loop fusion | flops 9156096 | bytes 217088 | tf_op jit(solution)/shard_map/reduce_sum | solution.py:30
  143.5 0.2 fusion.33
  143.7 0.1 mul.54
  143.8 0.0 slice-start.3
  143.8 4.7 %multiply_convert_fusion.5 = (bf16[16,160,192]{2,1,0:T(8,128)(2,1)S(1)}, bf16[16,160,192]{2,1,0:T(8,128)(2,1)S(1)}) fusion(f32[16,160,576]{2,1,0:T(8,128)} %copy-done, f32[16,160]{1,0:T(8,128)S(1)} %mul.54), kind=kLoop, calls=%fused_computation.21 | loop fusion | flops 6881280 | bytes 7874560 | tf_op jit(solution)/shard_map/convert_element_type | solution.py:69
  148.5 0.0 slice-start.4
  148.6 3.6 %fusion.36 = f32[16,160,768]{2,1,0:T(8,128)S(1)} fusion(bf16[16,160,192]{2,1,0:T(8,128)(2,1)S(1)} %get-tuple-element.40, bf16[16,768,192]{1,2,0:T(8,128)(2,1)} %param.11), kind=kOutput, calls=%fused_computation.54 | convolution fusion | flops 754974720 | bytes 13565952 | tf_op jit(solution)/shard_map/jrf,jdf->jrd/dot_general | solution.py:70
  152.1 0.0 slice-done.3
  152.1 0.0 slice-done.4
  152.2 1.3 add_convert_fusion
  153.4 3.7 %bitcast_convert_fusion = bf16[2,512,768]{2,1,0:T(8,128)(2,1)} fusion(bf16[16,2,80,768]{3,2,1,0:T(8,128)(2,1)S(1)} %bitcast.57, s32[2,16,512]{2,1,0:T(8,128)S(1)} %fusion.29), kind=kOutput, calls=%fused_computation.15 | convolution fusion | flops 2015363072 | bytes 5570560 | tf_op jit(solution)/shard_map/gest,egsd->gtd/dot_general | solution.py:74
  157.1 2.6 %copy.75 = bf16[1024,768]{0,1:T(8,128)(2,1)} copy(bf16[1024,768]{1,0:T(8,128)(2,1)} %bitcast.59) | data formatting | bytes 3145728 | tf_op jit(solution)/shard_map/reshape | solution.py:79
  159.7 2.7 %pad_maximum_fusion.1 = bf16[1024,776]{0,1:T(8,128)(2,1)} fusion(bf16[1024,8]{0,1:T(8,128)(2,1)S(1)} %fusion.33, bf16[1024,768]{0,1:T(8,128)(2,1)} %copy.75), kind=kLoop, calls=%fused_computation.37 | loop fusion | flops 3178496 | bytes 3178496 | tf_op jit(solution)/shard_map/concatenate | solution.py:85
  162.4 3.7 %copy.80 = bf16[1024,776]{1,0:T(8,128)(2,1)} copy(bf16[1024,776]{0,1:T(8,128)(2,1)} %pad_maximum_fusion.1) | data formatting | bytes 3178496
  166.1 0.0 reduce-scatter.4.cloned.1.call-update
  166.1 0.0 slice-start
  166.1 5.9 %convolution_convert_fusion.1 = bf16[16,768,192]{1,2,0:T(8,128)(2,1)} fusion(bf16[16,160,192]{2,1,0:T(8,128)(2,1)S(1)} %get-tuple-element.40, bf16[16,160,1536]{2,1,0:T(8,128)(2,1)} %bitcast.50), kind=kOutput, calls=%fused_computation.18 | convolution fusion | flops 757334016 | bytes 9633792 | tf_op jit(solution)/shard_map/jrd,jrf->jdf/dot_general | solution.py:90
  172.0 0.0 slice-start.1
  172.0 0.0 copy-start.2
  172.0 5.9 %convolution_convert_fusion = bf16[16,768,192]{1,2,0:T(8,128)(2,1)} fusion(bf16[16,160,192]{2,1,0:T(8,128)(2,1)S(1)} %get-tuple-element.39, bf16[16,160,1536]{2,1,0:T(8,128)(2,1)} %bitcast.51), kind=kOutput, calls=%fused_computation.17 | convolution fusion | flops 757334016 | bytes 9633792 | tf_op jit(solution)/shard_map/jrd,jrf->jdf/dot_general | solution.py:91
  178.0 0.0 slice-done
  178.0 0.0 slice-done.1
  178.0 0.0 copy-done.2
  178.0 3.5 %fusion.8 = bf16[16,192,768]{2,1,0:T(8,128)(2,1)} fusion(bf16[16,160,192]{2,1,0:T(8,128)(2,1)S(1)} %copy-done.2, f32[16,160]{1,0:T(8,128)S(1)} %mul.54, bf16[16,160,1536]{2,1,0:T(8,128)(2,1)S(1)} %bitcast.54), kind=kOutput, calls=%fused_computation.16 | convolution fusion | flops 763232256 | bytes 9977856 | tf_op jit(solution)/shard_map/jrf,jrd->jfd/dot_general | solution.py:93
  181.5 52.0 %reduce-scatter.4.cloned.1.call-done = bf16[128,776]{1,0:T(8,128)(2,1)} async-done(((bf16[1024,776]{1,0:T(8,128)(2,1)}), bf16[128,776]{1,0:T(8,128)(2,1)}) %reduce-scatter.4.cloned.1.call-update) | async-done | bytes 198672
  233.5 0.8 slice.49
  234.2 0.1 copy.83
  234.3 0.6 convert_element_type.83
  234.9 1.6 slice.48
  (7 shorter events, 0.0 us)
Async XLA Ops:
  7.2 70.7 %all-gather.2.cloned.1.call-start = ((), (), s32[]{:S(2)}) async-start(), calls=%async_computation.1 | async-start | bytes 3575808 | tf_op jit(solution)/shard_map/all_gather | solution.py:43
  11.6 123.6 %all-reduce.2.cloned.1.call-start = ((), (), s32[]{:S(2)}) async-start(), calls=%async_computation.2 | async-start | bytes 6553600 | tf_op jit(solution)/shard_map/psum | solution.py:61
  78.7 1.9 slice-start.2
  95.5 11.1 %copy-start.1 = (bf16[16,2,80,1536]{3,2,1,0:T(8,128)(2,1)}, bf16[16,2,80,1536]{3,2,1,0:T(8,128)(2,1)S(1)}, u32[]{:S(2)}) copy-start(bf16[16,2,80,1536]{3,2,1,0:T(8,128)(2,1)S(1)} %copy.71) | copy-start | bytes 23592964
  113.4 120.1 %reduce-scatter.4.cloned.1.call-start = ((), (), s32[]{:S(2)}) async-start(), calls=%async_computation.3 | async-start | bytes 2064384
  137.8 3.2 %copy-start = (f32[16,160,576]{2,1,0:T(8,128)}, f32[16,160,576]{2,1,0:T(8,128)S(1)}, u32[]{:S(2)}) copy-start(f32[16,160,576]{2,1,0:T(8,128)S(1)} %convert_element_type.75) | copy-start | bytes 17694724
  143.8 8.3 %slice-start.3 = ((s8[4718592]{0:T(1024)(128)(4,1)}), s8[4194304]{0:T(1024)(128)(4,1)S(1)}, s32[]{:S(2)}) async-start(s8[4718592]{0:T(1024)(128)(4,1)} %bitcast.55), calls=%async_computation.7 | async-start | bytes 8388608
  148.5 3.6 %slice-start.4 = ((s8[4718592]{0:T(1024)(128)(4,1)}), s8[524288]{0:T(1024)(128)(4,1)S(1)}, s32[]{:S(2)}) async-start(s8[4718592]{0:T(1024)(128)(4,1)} %bitcast.55), calls=%async_computation.8 | async-start | bytes 1048576
  166.1 11.9 %slice-start = ((s8[7864320]{0:T(1024)(128)(4,1)}), s8[4194304]{0:T(1024)(128)(4,1)S(1)}, s32[]{:S(2)}) async-start(s8[7864320]{0:T(1024)(128)(4,1)} %bitcast.52), calls=%async_computation.4 | async-start | bytes 8388608
  172.0 5.9 %slice-start.1 = ((s8[7864320]{0:T(1024)(128)(4,1)}), s8[3670016]{0:T(1024)(128)(4,1)S(1)}, s32[]{:S(2)}) async-start(s8[7864320]{0:T(1024)(128)(4,1)} %bitcast.52), calls=%async_computation.5 | async-start | bytes 7340032
  172.0 5.9 %copy-start.2 = (bf16[16,160,192]{2,1,0:T(8,128)(2,1)S(1)}, bf16[16,160,192]{2,1,0:T(8,128)(2,1)}, u32[]{:S(2)}) copy-start(bf16[16,160,192]{2,1,0:T(8,128)(2,1)} %get-tuple-element.38) | copy-start | bytes 2949124
Sparse Core Ops, SparseCore 0:
  11.7 66.1 all-gather.1
  113.5 21.6 all-reduce.1
  166.2 67.2 reduce-scatter.3
where the time goes:
time: 244 us; the launch traced here: 243 us
  waiting for transfers between devices  140 us (57%)
  matrix products  47.4 us (19%)
  other arithmetic  21.9 us (9%)
  local copies, waits for them, and re-layouts  19.9 us (8%)
  between operations  14 us (6%)
    all_gather x1, waiting for transfers between devices, on_device(): packed = lax.all_gather(packed, ('expert', 'dp'), axis=0, tiled=True)  66.2 us
    unnamed x4, waiting for transfers between devices  52 us
    psum x1, waiting for transfers between devices, on_device(): sums = lax.psum(parts, 'inner').astype(F32)  21.5 us
    dot_general x1, matrix products, on_device(): jnp.einsum('gest,gtd->egsd', picked, both, preferred_element_type=F32)  8.22 us
    dot_general x1, matrix products, on_device(): jnp.einsum('jrd,jfd->jrf', expert_grads, down_weight, preferred_element_t...  6.93 us
    unnamed x18, local copies, waits for them, and re-layouts  6.4 us
    dot_general x1, matrix products, on_device(): jnp.einsum('jrd,jrf->jdf', expert_rows, gate_back, preferred_element_type...  5.93 us
    dot_general x1, matrix products, on_device(): jnp.einsum('jrd,jrf->jdf', expert_rows, up_back, preferred_element_type=F32)  5.92 us
  transfers between devices with their start and end apart: 3, of which 3 were waited for; matrix products, arithmetic and copies ran while one was open for 6% of the time, Pallas kernels for 0%

commit v1 on v0

--- a/solution.py
+++ b/solution.py
@@ -58,7 +58,7 @@
         ],
         axis=2,
     ).astype(BF16)
-    sums = lax.psum(parts, "inner").astype(F32)
+    sums = jnp.sum(lax.all_gather(parts, "inner"), axis=0).astype(F32)
     gate, up, slope = (sums[..., :hid], sums[..., hid : 2 * hid], sums[..., 2 * hid :])
     sig = jax.nn.sigmoid(gate)
     act = gate * sig

time: 244 us -> 241 us (0.988)
  waiting for transfers between devices: 140 us -> 133 us
  other arithmetic: 21.9 us -> 25.4 us
    psum x1 -> x0, waiting for transfers between devices: 21.5 us -> none  [on_device(): sums = lax.psum(parts, 'inner').astype(F32)]
    all_gather x0 -> x1, waiting for transfers between devices: none -> 15.1 us  [on_device(): sums = jnp.sum(lax.all_gather(parts, 'inner'), axis=0).astype(F32)]
    reduce_sum x0 -> x1, other arithmetic: none -> 5.61 us  [on_device(): sums = jnp.sum(lax.all_gather(parts, 'inner'), axis=0).astype(F32)]
where the time goes in v1:
time: 241 us; the launch traced here: 240 us
  waiting for transfers between devices  133 us (55%)
  matrix products  47.4 us (20%)
  other arithmetic  25.4 us (11%)
  local copies, waits for them, and re-layouts  19.9 us (8%)
  between operations  14 us (6%)
    all_gather x1, waiting for transfers between devices, on_device(): packed = lax.all_gather(packed, ('expert', 'dp'), axis=0, tiled=True)  66.2 us
    unnamed x4, waiting for transfers between devices  52.1 us
    all_gather x1, waiting for transfers between devices, on_device(): sums = jnp.sum(lax.all_gather(parts, 'inner'), axis=0).astype(F32)  15.1 us
    dot_general x1, matrix products, on_device(): jnp.einsum('gest,gtd->egsd', picked, both, preferred_element_type=F32)  8.22 us
    dot_general x1, matrix products, on_device(): jnp.einsum('jrd,jfd->jrf', expert_grads, down_weight, preferred_element_t...  6.93 us
    unnamed x18, local copies, waits for them, and re-layouts  6.4 us
    dot_general x1, matrix products, on_device(): jnp.einsum('jrd,jrf->jdf', expert_rows, gate_back, preferred_element_type...  5.93 us
    dot_general x1, matrix products, on_device(): jnp.einsum('jrd,jrf->jdf', expert_rows, up_back, preferred_element_type=F32)  5.92 us
  transfers between devices with their start and end apart: 3, of which 3 were waited for; matrix products, arithmetic and copies ran while one was open for 6% of the time, Pallas kernels for 0%

profile of v1, /device:TPU:0, one launch (start us, length us, event | category | flops | bytes accessed | tf_op | source)
XLA Modules:
  0.0 240.4 jit_solution(10522363143159193512)
XLA Ops:
  7.2 0.0 all-gather.3.cloned.1.call-start
  7.2 0.7 convert_element_type.78
  7.9 0.7 convert_element_type.77
  8.6 1.1 copy.65
  9.7 1.1 copy.64
  10.8 0.8 pad_maximum_fusion.2
  11.6 0.0 all-gather.3.cloned.1.call-update
  11.6 0.0 all-gather.5.cloned.1.call-start
  11.6 66.2 %all-gather.3.cloned.1.call-done = bf16[1024,1552]{0,1:T(8,128)(2,1)} async-done(((bf16[128,1552]{0,1:T(8,128)(2,1)}), bf16[1024,1552]{0,1:T(8,128)(2,1)}) %all-gather.3.cloned.1.call-update) | async-done | bytes 3178512 | tf_op jit(solution)/shard_map/all_gather | solution.py:43
  77.9 0.7 slice_convert_fusion.1
  78.6 0.1 compare_reduce_fusion
  78.7 0.0 slice-start.2
  78.8 0.3 fusion.38
  79.0 1.6 slice-done.2
  80.6 2.9 %copy.79 = bf16[1024,1536]{1,0:T(8,128)(2,1)} copy(bf16[1024,1536]{0,1:T(8,128)(2,1)S(1)} %slice-done.2) | data formatting | bytes 6291456 | tf_op jit(solution)/shard_map/reshape | solution.py:47
  83.6 8.2 %convert_bitcast_fusion = bf16[16,2,80,1536]{3,2,0,1:T(8,128)(2,1)} fusion(bf16[2,512,1536,1]{2,1,3,0:T(8,128)(2,1)} %bitcast.64, s32[2,16,512]{2,1,0:T(8,128)S(1)} %fusion.38), kind=kOutput, calls=%fused_computation.2 | convolution fusion | flops 4031774720 | bytes 11075584 | tf_op jit(solution)/shard_map/gest,gtd->egsd/dot_general | solution.py:48
  91.8 3.7 %copy.71 = bf16[16,2,80,1536]{3,2,1,0:T(8,128)(2,1)S(1)} copy(bf16[16,2,80,1536]{3,2,0,1:T(8,128)(2,1)} %convert_bitcast_fusion) | data formatting | bytes 15728640 | tf_op jit(solution)/shard_map/convert_element_type | solution.py:49
  95.5 0.0 copy-start.1
  95.5 6.9 %fusion.29 = bf16[1,16,160,192]{3,2,1,0:T(8,128)(2,1)S(1)} fusion(bf16[16,192,768]{2,1,0:T(8,128)(2,1)} %param.13, bf16[16,160,1536]{2,1,0:T(8,128)(2,1)S(1)} %bitcast.53), kind=kOutput, calls=%fused_computation.38 | convolution fusion | flops 755466240 | bytes 9633792 | tf_op jit(solution)/shard_map/jrd,jfd->jrf/dot_general | solution.py:57
  102.5 4.1 %fusion.32 = bf16[1,16,160,192]{3,2,1,0:T(8,128)(2,1)S(1)} fusion(bf16[16,768,192]{1,2,0:T(8,128)(2,1)} %param.12, bf16[16,160,1536]{2,1,0:T(8,128)(2,1)S(1)} %bitcast.54), kind=kOutput, calls=%fused_computation.39 | convolution fusion | flops 755466240 | bytes 9633792 | tf_op jit(solution)/shard_map/jrd,jdf->jrf/dot_general | solution.py:56
  106.6 0.0 copy-done.1
  106.6 4.0 %fusion.35 = bf16[1,16,160,192]{3,2,1,0:T(8,128)(2,1)S(1)} fusion(bf16[16,768,192]{1,2,0:T(8,128)(2,1)} %param.11, bf16[16,160,1536]{2,1,0:T(8,128)(2,1)S(1)} %bitcast.55), kind=kOutput, calls=%fused_computation.40 | convolution fusion | flops 755466240 | bytes 9633792 | tf_op jit(solution)/shard_map/jrd,jdf->jrf/dot_general | solution.py:55
  110.6 2.8 %pad_maximum_fusion = bf16[1,16,160,576]{3,2,1,0:T(8,128)(2,1)} fusion(bf16[1,16,160,192]{3,2,1,0:T(8,128)(2,1)S(1)} %fusion.29, bf16[1,16,160,192]{3,2,1,0:T(8,128)(2,1)S(1)} %fusion.32, bf16[1,16,160,192]{3,2,1,0:T(8,128)(2,1)S(1)} %fusion.35), kind=kLoop, calls=%fused_computation.14 | loop fusion | flops 8847360 | bytes 5898240 | tf_op jit(solution)/shard_map/concatenate | solution.py:53
  113.4 0.0 all-gather.5.cloned.1.call-update
  113.4 0.2 reduce-scatter.4.cloned.1.call-start
  113.7 0.1 fusion.41
  113.8 0.1 reshape.92
  113.9 15.1 %all-gather.5.cloned.1.call-done = bf16[2,16,160,576]{3,2,1,0:T(8,128)(2,1)} async-done(((bf16[1,16,160,576]{3,2,1,0:T(8,128)(2,1)}), bf16[2,16,160,576]{3,2,1,0:T(8,128)(2,1)}) %all-gather.5.cloned.1.call-update) | async-done | bytes 5898256 | tf_op jit(solution)/shard_map/all_gather | solution.py:61
  128.9 5.6 %reduce_sum.59 = bf16[16,160,576]{2,1,0:T(8,128)(2,1)S(1)} reduce(bf16[2,16,160,576]{3,2,1,0:T(8,128)(2,1)} %all-gather.5.cloned.1.call-done, bf16[]{:T(256)} %constant.15.clone.1), dimensions={0}, to_apply=%region_3.4 | reduce | flops 1474560 | bytes 8847362 | tf_op jit(solution)/shard_map/reduce_sum | solution.py:61
  134.5 0.6 convert_element_type.84
  135.2 0.0 copy-start
  135.2 2.7 %multiply_reduce_fusion.1 = (f32[16,160]{1,0:T(8,128)S(1)}, bf16[16,160,192]{2,1,0:T(8,128)(2,1)}) fusion(f32[16,160,576]{2,1,0:T(8,128)S(1)} %convert_element_type.84), kind=kLoop, calls=%fused_computation.19 | loop fusion | flops 4421120 | bytes 6891520 | tf_op jit(solution)/shard_map/reduce_sum | solution.py:66
  137.9 0.4 copy-done
  138.4 0.1 reshape.97
  138.4 2.3 select_reduce_fusion
  140.7 0.2 fusion.42
  140.9 0.1 mul.54
  141.0 0.0 slice-start.3
  141.0 4.7 %multiply_convert_fusion.5 = (bf16[16,160,192]{2,1,0:T(8,128)(2,1)S(1)}, bf16[16,160,192]{2,1,0:T(8,128)(2,1)S(1)}) fusion(f32[16,160,576]{2,1,0:T(8,128)} %copy-done, f32[16,160]{1,0:T(8,128)S(1)} %mul.54), kind=kLoop, calls=%fused_computation.21 | loop fusion | flops 6881280 | bytes 7874560 | tf_op jit(solution)/shard_map/convert_element_type | solution.py:69
  145.7 0.0 slice-start.4
  145.8 3.6 %fusion.45 = f32[16,160,768]{2,1,0:T(8,128)S(1)} fusion(bf16[16,160,192]{2,1,0:T(8,128)(2,1)S(1)} %get-tuple-element.40, bf16[16,768,192]{1,2,0:T(8,128)(2,1)} %param.11), kind=kOutput, calls=%fused_computation.57 | convolution fusion | flops 754974720 | bytes 13565952 | tf_op jit(solution)/shard_map/jrf,jdf->jrd/dot_general | solution.py:70
  149.3 0.0 slice-done.3
  149.3 0.0 slice-done.4
  149.4 1.3 add_convert_fusion
  150.6 3.7 %bitcast_convert_fusion = bf16[2,512,768]{2,1,0:T(8,128)(2,1)} fusion(bf16[16,2,80,768]{3,2,1,0:T(8,128)(2,1)S(1)} %bitcast.63, s32[2,16,512]{2,1,0:T(8,128)S(1)} %fusion.38), kind=kOutput, calls=%fused_computation.15 | convolution fusion | flops 2015363072 | bytes 5570560 | tf_op jit(solution)/shard_map/gest,egsd->gtd/dot_general | solution.py:74
  154.3 2.6 %copy.75 = bf16[1024,768]{0,1:T(8,128)(2,1)} copy(bf16[1024,768]{1,0:T(8,128)(2,1)} %bitcast.65) | data formatting | bytes 3145728 | tf_op jit(solution)/shard_map/reshape | solution.py:79
  156.9 2.7 %pad_maximum_fusion.1 = bf16[1024,776]{0,1:T(8,128)(2,1)} fusion(bf16[1024,8]{0,1:T(8,128)(2,1)S(1)} %fusion.42, bf16[1024,768]{0,1:T(8,128)(2,1)} %copy.75), kind=kLoop, calls=%fused_computation.37 | loop fusion | flops 3178496 | bytes 3178496 | tf_op jit(solution)/shard_map/concatenate | solution.py:85
  159.6 3.7 %copy.80 = bf16[1024,776]{1,0:T(8,128)(2,1)} copy(bf16[1024,776]{0,1:T(8,128)(2,1)} %pad_maximum_fusion.1) | data formatting | bytes 3178496
  163.3 0.0 reduce-scatter.4.cloned.1.call-update
  163.3 0.0 slice-start
  163.3 5.9 %convolution_convert_fusion.1 = bf16[16,768,192]{1,2,0:T(8,128)(2,1)} fusion(bf16[16,160,192]{2,1,0:T(8,128)(2,1)S(1)} %get-tuple-element.40, bf16[16,160,1536]{2,1,0:T(8,128)(2,1)} %bitcast.56), kind=kOutput, calls=%fused_computation.18 | convolution fusion | flops 757334016 | bytes 9633792 | tf_op jit(solution)/shard_map/jrd,jrf->jdf/dot_general | solution.py:90
  169.2 0.0 slice-start.1
  169.2 0.0 copy-start.2
  169.2 5.9 %convolution_convert_fusion = bf16[16,768,192]{1,2,0:T(8,128)(2,1)} fusion(bf16[16,160,192]{2,1,0:T(8,128)(2,1)S(1)} %get-tuple-element.39, bf16[16,160,1536]{2,1,0:T(8,128)(2,1)} %bitcast.57), kind=kOutput, calls=%fused_computation.17 | convolution fusion | flops 757334016 | bytes 9633792 | tf_op jit(solution)/shard_map/jrd,jrf->jdf/dot_general | solution.py:91
  175.2 0.0 slice-done
  175.2 0.0 slice-done.1
  175.2 0.0 copy-done.2
  175.2 3.5 %fusion.8 = bf16[16,192,768]{2,1,0:T(8,128)(2,1)} fusion(bf16[16,160,192]{2,1,0:T(8,128)(2,1)S(1)} %copy-done.2, f32[16,160]{1,0:T(8,128)S(1)} %mul.54, bf16[16,160,1536]{2,1,0:T(8,128)(2,1)S(1)} %bitcast.60), kind=kOutput, calls=%fused_computation.16 | convolution fusion | flops 763232256 | bytes 9977856 | tf_op jit(solution)/shard_map/jrf,jrd->jfd/dot_general | solution.py:93
  178.7 52.1 %reduce-scatter.4.cloned.1.call-done = bf16[128,776]{1,0:T(8,128)(2,1)} async-done(((bf16[1024,776]{1,0:T(8,128)(2,1)}), bf16[128,776]{1,0:T(8,128)(2,1)}) %reduce-scatter.4.cloned.1.call-update) | async-done | bytes 198672
  230.8 0.8 slice.49
  231.5 0.1 copy.83
  231.6 0.6 convert_element_type.92
  232.2 1.6 slice.48
  (7 shorter events, 0.0 us)
Async XLA Ops:
  7.2 70.7 %all-gather.3.cloned.1.call-start = ((), (), s32[]{:S(2)}) async-start(), calls=%async_computation.1 | async-start | bytes 3575808 | tf_op jit(solution)/shard_map/all_gather | solution.py:43
  11.6 117.3 %all-gather.5.cloned.1.call-start = ((), (), s32[]{:S(2)}) async-start(), calls=%async_computation.2 | async-start | bytes 9830400 | tf_op jit(solution)/shard_map/all_gather | solution.py:61
  78.7 1.9 slice-start.2
  95.5 11.1 %copy-start.1 = (bf16[16,2,80,1536]{3,2,1,0:T(8,128)(2,1)}, bf16[16,2,80,1536]{3,2,1,0:T(8,128)(2,1)S(1)}, u32[]{:S(2)}) copy-start(bf16[16,2,80,1536]{3,2,1,0:T(8,128)(2,1)S(1)} %copy.71) | copy-start | bytes 23592964
  113.4 117.3 %reduce-scatter.4.cloned.1.call-start = ((), (), s32[]{:S(2)}) async-start(), calls=%async_computation.3 | async-start | bytes 2064384
  135.2 3.2 %copy-start = (f32[16,160,576]{2,1,0:T(8,128)}, f32[16,160,576]{2,1,0:T(8,128)S(1)}, u32[]{:S(2)}) copy-start(f32[16,160,576]{2,1,0:T(8,128)S(1)} %convert_element_type.84) | copy-start | bytes 17694724
  141.0 8.3 %slice-start.3 = ((s8[4718592]{0:T(1024)(128)(4,1)}), s8[4194304]{0:T(1024)(128)(4,1)S(1)}, s32[]{:S(2)}) async-start(s8[4718592]{0:T(1024)(128)(4,1)} %bitcast.61), calls=%async_computation.7 | async-start | bytes 8388608
  145.7 3.6 %slice-start.4 = ((s8[4718592]{0:T(1024)(128)(4,1)}), s8[524288]{0:T(1024)(128)(4,1)S(1)}, s32[]{:S(2)}) async-start(s8[4718592]{0:T(1024)(128)(4,1)} %bitcast.61), calls=%async_computation.8 | async-start | bytes 1048576
  163.3 11.9 %slice-start = ((s8[7864320]{0:T(1024)(128)(4,1)}), s8[4194304]{0:T(1024)(128)(4,1)S(1)}, s32[]{:S(2)}) async-start(s8[7864320]{0:T(1024)(128)(4,1)} %bitcast.58), calls=%async_computation.4 | async-start | bytes 8388608
  169.2 5.9 %slice-start.1 = ((s8[7864320]{0:T(1024)(128)(4,1)}), s8[3670016]{0:T(1024)(128)(4,1)S(1)}, s32[]{:S(2)}) async-start(s8[7864320]{0:T(1024)(128)(4,1)} %bitcast.58), calls=%async_computation.5 | async-start | bytes 7340032
  169.2 5.9 %copy-start.2 = (bf16[16,160,192]{2,1,0:T(8,128)(2,1)S(1)}, bf16[16,160,192]{2,1,0:T(8,128)(2,1)}, u32[]{:S(2)}) copy-start(bf16[16,160,192]{2,1,0:T(8,128)(2,1)} %get-tuple-element.38) | copy-start | bytes 2949124
Sparse Core Ops, SparseCore 0:
  11.7 66.1 all-gather.2
  113.5 15.3 all-gather.4
  163.4 67.2 reduce-scatter.3
